TPU v7x, 32 devices: a whole 2x2x4 slice. The times are simulated.
32 devices in a mesh: rows: 8 (over z, x), cols: 4 (over y, core).
Axes of the slice: x: 2, y: 2, z: 4, core: 2. Of those that a mesh axis runs over, the one named last changes fastest.
Arguments:
- query: bfloat16 [24, 256, 2048], P('rows', 'cols'), may hold values from -6 to 6
- key: bfloat16 [24, 256, 2048], P('rows', 'cols'), may hold values from -6 to 6
- value: bfloat16 [24, 256, 2048], P('rows', 'cols'), may hold values from -6 to 6
- cotangent: bfloat16 [24, 256, 2048], P('rows', 'cols'), may hold values from -6 to 6
- conv_weight: bfloat16 [9, 2048], replicated, may hold values from -1.1953125 to 1.1953125
- row_mask: int32 [24, 2, 2], P('rows'), may hold values from 0 to 1, as said below
- col_mask: int32 [256, 3, 3], P('cols'), may hold values from 0 to 1, as said below
Outputs:
- out: bfloat16 [24, 256, 2048], P('rows', 'cols')
- dquery: bfloat16 [24, 256, 2048], P('rows', 'cols')
- dkey: bfloat16 [24, 256, 2048], P('rows', 'cols')
- dvalue: bfloat16 [24, 256, 2048], P('rows', 'cols')
Inputs may be any that keep to these rules, and one draw needn't show every extreme that they name: `row_mask`: every diagonal block is 1: a query block always sees its own block. `col_mask`: every diagonal block is 1: a query block always sees its own block.
All inputs are finite; a program needn't handle non-finite values.
Results may differ from a plain program's by a relative error of at most 0.011.
Values may be sent and summed in bfloat16 or wider, within the bound.
A program may use at most 128 MiB of HBM per device.

v0:
```python
import math
import jax
import jax.numpy as jnp
from jax import lax
from jax.sharding import PartitionSpec as P

HEAD_DIM = 128
SHEET_ROW_BLOCKS = 2
COL_BLOCKS = 3


def padded(array, sides, width):
    for axis, dim in sides:
        devices, length = (lax.axis_size(axis), array.shape[dim])
        up = [(i, (i + 1) % devices) for i in range(devices - 1)]
        down = [(j, i) for i, j in up]
        last = lax.slice_in_dim(array, length - width, length, axis=dim)
        leading = lax.slice_in_dim(array, 0, width, axis=dim)
        before = lax.ppermute(last, axis, up)
        after = lax.ppermute(leading, axis, down)
        array = jnp.concatenate([before, array, after], axis=dim)
    return array


def block_allow(block_mask_table, query_pos, key_pos, block_len, block_count):
    labels = jnp.arange(block_count)
    query_onehot_rows = (query_pos[:, None] // block_len == labels[None, :]).astype(jnp.float32)
    key_onehot_rows = (key_pos[:, None] // block_len == labels[None, :]).astype(jnp.float32)
    merged_links = jnp.einsum(
        "xv,zvs,hs->zxh", query_onehot_rows, block_mask_table.astype(jnp.float32), key_onehot_rows
    )
    return merged_links > 0.5


def line_attention(query_part, key_part, value_part, grad_part, allowed, layout):
    if layout == "bq":
        query_form = "bqhd"
        key_layout_shape = "bkhd"
    else:
        query_form = "qbhd"
        key_layout_shape = "kbhd"
    score_scale = 1.0 / math.sqrt(query_part.shape[-1])
    pair_form = query_form + "," + key_layout_shape + "->bhqk"
    scores = (
        jnp.einsum(pair_form, query_part, key_part, preferred_element_type=jnp.float32)
        * score_scale
    )
    scores = jnp.where(allowed[:, None], scores, -jnp.inf)
    highest = jnp.max(scores, axis=-1, keepdims=True)
    weights = jnp.exp(scores - highest)
    weights = weights / jnp.sum(weights, axis=-1, keepdims=True)
    rounded = weights.astype(jnp.bfloat16)
    attended = jnp.einsum(
        "bhqk," + key_layout_shape + "->" + query_form,
        rounded,
        value_part,
        preferred_element_type=jnp.float32,
    )
    dweights = jnp.einsum(pair_form, grad_part, value_part, preferred_element_type=jnp.float32)
    delta = jnp.sum(grad_part.astype(jnp.float32) * attended, axis=-1)
    if layout == "bq":
        delta = jnp.transpose(delta, (0, 2, 1))
    else:
        delta = jnp.transpose(delta, (1, 2, 0))
    dscores = (weights * (dweights - delta[..., None]) * score_scale).astype(jnp.bfloat16)
    dquery = jnp.einsum(
        "bhqk," + key_layout_shape + "->" + query_form,
        dscores,
        key_part,
        preferred_element_type=jnp.float32,
    )
    dkey = jnp.einsum(
        "bhqk," + query_form + "->" + key_layout_shape,
        dscores,
        query_part,
        preferred_element_type=jnp.float32,
    )
    dvalue = jnp.einsum(
        "bhqk," + query_form + "->" + key_layout_shape,
        rounded,
        grad_part,
        preferred_element_type=jnp.float32,
    )
    return (attended, dquery, dkey, dvalue)


def depthwise(padded_field, taps, rows_count, cols_count, reverse_taps):
    summed = jnp.zeros((rows_count, cols_count, taps.shape[1]), jnp.float32)
    for row_offset_start in range(3):
        for offset_col in range(3):
            if reverse_taps:
                start_row = 2 - row_offset_start
                start_col = 2 - offset_col
            else:
                start_row = row_offset_start
                start_col = offset_col
            window = padded_field[
                start_row : start_row + rows_count, start_col : start_col + cols_count
            ]
            summed = summed + taps[row_offset_start * 3 + offset_col] * window.astype(jnp.float32)
    return summed


def body(query, key, value, cotangent, conv_weight, row_mask, col_mask):
    rows_here, cols_here, width = query.shape
    half_width = width // 2
    head_groups = half_width // HEAD_DIM
    row_devices = lax.axis_size("rows")
    col_devices = lax.axis_size("cols")
    sheet_rows = rows_here * row_devices
    sheet_cols = cols_here * col_devices
    taps = conv_weight.astype(jnp.float32)
    padded_value = padded(value, (("rows", 0), ("cols", 1)), 1)
    padded_grad = padded(cotangent, (("rows", 0), ("cols", 1)), 1)
    row_len = sheet_cols // SHEET_ROW_BLOCKS
    keys_row, values_row = (
        lax.all_gather(key[:, :, :half_width], "cols", axis=1, tiled=True),
        lax.all_gather(value[:, :, :half_width], "cols", axis=1, tiled=True),
    )
    col_start = lax.axis_index("cols") * cols_here
    allowed = block_allow(
        row_mask,
        col_start + jnp.arange(cols_here),
        jnp.arange(sheet_cols),
        row_len,
        SHEET_ROW_BLOCKS,
    )
    local_shape = (rows_here, cols_here, head_groups, HEAD_DIM)
    whole_shape = (rows_here, sheet_cols, head_groups, HEAD_DIM)
    results = line_attention(
        query[:, :, :half_width].reshape(local_shape),
        keys_row.reshape(whole_shape),
        values_row.reshape(whole_shape),
        cotangent[:, :, :half_width].reshape(local_shape),
        allowed,
        "bq",
    )
    key_terms = results[2].reshape(rows_here, sheet_cols, half_width)
    value_terms = results[3].reshape(rows_here, sheet_cols, half_width)
    key_grads, value_grads = (
        lax.psum_scatter(key_terms, "cols", scatter_dimension=1, tiled=True),
        lax.psum_scatter(value_terms, "cols", scatter_dimension=1, tiled=True),
    )
    out_row = results[0].reshape(rows_here, cols_here, half_width).astype(jnp.bfloat16)
    dq_row = results[1].reshape(rows_here, cols_here, half_width).astype(jnp.bfloat16)
    dk_row = key_grads.astype(jnp.bfloat16)
    dv_row = value_grads.astype(jnp.bfloat16)
    columns_each = cols_here // row_devices
    moved = (
        lax.all_to_all(query[:, :, half_width:], "rows", split_axis=1, concat_axis=0, tiled=True),
        lax.all_to_all(key[:, :, half_width:], "rows", split_axis=1, concat_axis=0, tiled=True),
        lax.all_to_all(value[:, :, half_width:], "rows", split_axis=1, concat_axis=0, tiled=True),
        lax.all_to_all(
            cotangent[:, :, half_width:], "rows", split_axis=1, concat_axis=0, tiled=True
        ),
    )
    column_shape = (sheet_rows, columns_each, head_groups, HEAD_DIM)
    my_tables = lax.dynamic_slice_in_dim(
        col_mask, lax.axis_index("rows") * columns_each, columns_each, 0
    )
    col_len = sheet_rows // COL_BLOCKS
    positions = jnp.arange(sheet_rows)
    col_allowed = block_allow(my_tables, positions, positions, col_len, COL_BLOCKS)
    col_results = line_attention(
        moved[0].reshape(column_shape),
        moved[1].reshape(column_shape),
        moved[2].reshape(column_shape),
        moved[3].reshape(column_shape),
        col_allowed,
        "qb",
    )
    column_flat = (sheet_rows, columns_each, half_width)
    col_pieces = [piece.reshape(column_flat).astype(jnp.bfloat16) for piece in col_results]
    out_col, dq_col, dk_col, dv_col = (
        lax.all_to_all(col_pieces[0], "rows", split_axis=0, concat_axis=1, tiled=True),
        lax.all_to_all(col_pieces[1], "rows", split_axis=0, concat_axis=1, tiled=True),
        lax.all_to_all(col_pieces[2], "rows", split_axis=0, concat_axis=1, tiled=True),
        lax.all_to_all(col_pieces[3], "rows", split_axis=0, concat_axis=1, tiled=True),
    )
    lepe = depthwise(padded_value, taps, rows_here, cols_here, False)
    back_conv = depthwise(padded_grad, taps, rows_here, cols_here, True)
    attended16 = jnp.concatenate([out_row, out_col], axis=2)
    out = (attended16.astype(jnp.float32) + lepe).astype(jnp.bfloat16)
    dquery = jnp.concatenate([dq_row, dq_col], axis=2)
    dkey = jnp.concatenate([dk_row, dk_col], axis=2)
    dvalue_attn = jnp.concatenate([dv_row, dv_col], axis=2)
    dvalue = (dvalue_attn.astype(jnp.float32) + back_conv).astype(jnp.bfloat16)
    return (out, dquery, dkey, dvalue)


def solution(mesh):
    return jax.shard_map(
        body,
        mesh=mesh,
        in_specs=(
            P("rows", "cols", None),
            P("rows", "cols", None),
            P("rows", "cols", None),
            P("rows", "cols", None),
            P(),
            P("rows", None, None),
            P("cols", None, None),
        ),
        out_specs=(
            P("rows", "cols", None),
            P("rows", "cols", None),
            P("rows", "cols", None),
            P("rows", "cols", None),
        ),
        check_vma=False,
    )
```

profile of v0, /device:TPU:1, one launch (start us, length us, event | category | flops | bytes accessed | tf_op | source)
XLA Modules:
  0.0 257.9 jit_solution(13641217916702605888)
XLA Ops:
  7.2 2.2 fusion.64
  13.5 18.9 %all-gather.3.cloned.1.call-done = bf16[3,256,1024]{2,1,0:T(8,128)(2,1)} async-done(((bf16[3,64,1024]{2,1,0:T(8,128)(2,1)}), bf16[3,256,1024]{2,1,0:T(8,128)(2,1)}) %all-gather.3.cloned.1.call-update) | async-done | bytes 1572880 | tf_op jit(solution)/shard_map/all_gather | solution.py:117
  32.3 1.7 copy.100
  34.0 1.2 multiply_select_fusion
  35.2 1.2 copy-done.3
  36.4 2.1 fusion.69
  38.5 15.7 %all-gather.5.cloned.1.call-done = bf16[3,256,1024]{2,1,0:T(8,128)(2,1)} async-done(((bf16[3,64,1024]{2,1,0:T(8,128)(2,1)}), bf16[3,256,1024]{2,1,0:T(8,128)(2,1)}) %all-gather.5.cloned.1.call-update) | async-done | bytes 1572880 | tf_op jit(solution)/shard_map/all_gather | solution.py:118
  54.2 2.6 %copy.103 = bf16[3,256,1024]{1,2,0:T(8,128)(2,1)} copy(bf16[3,256,1024]{2,1,0:T(8,128)(2,1)} %all-gather.5.cloned.1.call-done) | data formatting | bytes 3145728 | tf_op jit(solution)/shard_map/all_gather | solution.py:118
  56.7 6.6 %multiply_reduce_fusion.1 = (f32[3,64,8]{1,2,0:T(8,128)}, bf16[3,8,8,8,128]{4,3,2,1,0:T(8,128)(2,1)}) fusion(bf16[3,8,8,8,128]{4,3,2,1,0:T(8,128)(2,1)} %get-tuple-element.12, bf16[3,256,8,128]{1,3,2,0:T(8,128)(2,1)} %bitcast.155, f32[3,8,64]{2,1,0:T(8,128)} %get-tuple-element.36, f32[3,8,64,256]{3,2,1,0:T(8,128)} %copy-done.3), kind=kOutput, calls=%fused_computation.64 | convolution fusion | flops 102629632 | bytes 3944448 | tf_op jit(solution)/shard_map/bhqk,bkhd->bqhd/dot_general | solution.py:53
  63.4 2.5 multiply_convert_fusion
  65.9 2.4 fusion.26
  68.2 3.5 %copy.137 = f32[3,256,1024]{2,1,0:T(8,128)} copy(f32[3,256,1024]{1,2,0:T(8,128)} %bitcast.153) | data formatting | bytes 6291456 | tf_op jit(solution)/shard_map/reshape | solution.py:138
  71.8 2.2 copy.154
  74.0 5.2 %all-to-all-start = ((bf16[3,64,1024]{2,0,1:T(4,128)(2,1)}), bf16[3,64,1024]{2,0,1:T(4,128)(2,1)}, u32[]{:S(2)}, u32[]{:S(2)}) async-start(bf16[3,64,1024]{2,0,1:T(4,128)(2,1)} %copy.154), calls=%async_computation | async-start | bytes 1048576 | tf_op jit(solution)/shard_map/all_to_all | solution.py:150
  79.2 1.1 copy.155
  80.4 12.7 %all-to-all-done = bf16[3,64,1024]{2,0,1:T(4,128)(2,1)} async-done(((bf16[3,64,1024]{2,0,1:T(4,128)(2,1)}), bf16[3,64,1024]{2,0,1:T(4,128)(2,1)}, u32[]{:S(2)}, u32[]{:S(2)}) %all-to-all-start) | async-done | bytes 393248 | tf_op jit(solution)/shard_map/all_to_all | solution.py:150
  93.1 4.6 %all-to-all-start.1 = ((bf16[3,64,1024]{2,0,1:T(4,128)(2,1)}), bf16[3,64,1024]{2,0,1:T(4,128)(2,1)}, u32[]{:S(2)}, u32[]{:S(2)}) async-start(bf16[3,64,1024]{2,0,1:T(4,128)(2,1)} %copy.155), calls=%async_computation.1 | async-start | bytes 1048576 | tf_op jit(solution)/shard_map/all_to_all | solution.py:151
  98.4 1.3 collective-permute-start.1
  99.7 4.7 %collective-permute-start = (bf16[1,64,2048]{2,1,0:T(8,128)(2,1)}, bf16[1,64,2048]{2,1,0:T(8,128)(2,1)}, u32[]{:S(2)}, u32[]{:S(2)}) collective-permute-start(bf16[1,64,2048]{2,1,0:T(8,128)(2,1)} %get-tuple-element.23), channel_id=1, source_target_pairs={{0,4},{4,8},{8,12},{12,16},{16,20},{20,24},{24,28},{1,5},{5,9},{9,... | collective-permute-start | bytes 786440 | tf_op jit(solution)/shard_map/ppermute | solution.py:19
  104.4 2.2 copy.156
  106.6 3.0 %all-to-all-done.1 = bf16[3,64,1024]{2,0,1:T(4,128)(2,1)} async-done(((bf16[3,64,1024]{2,0,1:T(4,128)(2,1)}), bf16[3,64,1024]{2,0,1:T(4,128)(2,1)}, u32[]{:S(2)}, u32[]{:S(2)}) %all-to-all-start.1) | async-done | bytes 393248 | tf_op jit(solution)/shard_map/all_to_all | solution.py:151
  109.6 6.3 %all-to-all-start.2 = ((bf16[3,64,1024]{2,0,1:T(4,128)(2,1)}), bf16[3,64,1024]{2,0,1:T(4,128)(2,1)}, u32[]{:S(2)}, u32[]{:S(2)}) async-start(bf16[3,64,1024]{2,0,1:T(4,128)(2,1)} %copy.156), calls=%async_computation.2 | async-start | bytes 1048576 | tf_op jit(solution)/shard_map/all_to_all | solution.py:152
  116.8 1.3 collective-permute-start.5
  118.0 4.7 %collective-permute-start.4 = (bf16[1,64,2048]{2,1,0:T(8,128)(2,1)}, bf16[1,64,2048]{2,1,0:T(8,128)(2,1)}, u32[]{:S(2)}, u32[]{:S(2)}) collective-permute-start(bf16[1,64,2048]{2,1,0:T(8,128)(2,1)} %get-tuple-element.9), channel_id=1, source_target_pairs={{0,4},{4,8},{8,12},{12,16},{16,20},{20,24},{24,28},{1,5},{5,9},{9,... | collective-permute-start | bytes 786440 | tf_op jit(solution)/shard_map/ppermute | solution.py:19
  123.8 1.4 copy.108
  125.3 1.1 copy.157
  126.4 6.6 %all-to-all-start.4 = ((bf16[3,64,1024]{2,0,1:T(4,128)(2,1)}), bf16[3,64,1024]{2,0,1:T(4,128)(2,1)}, u32[]{:S(2)}, u32[]{:S(2)}) async-start(bf16[3,64,1024]{2,0,1:T(4,128)(2,1)} %copy.157), calls=%async_computation.4 | async-start | bytes 1048576 | tf_op jit(solution)/shard_map/all_to_all | solution.py:153
  133.3 6.8 %fusion.23 = f32[3,8,256,128]{2,3,1,0:T(8,128)} fusion(bf16[3,8,8,8,128]{4,3,2,1,0:T(8,128)(2,1)} %get-tuple-element.12, f32[3,8,64]{2,1,0:T(8,128)} %get-tuple-element.36, f32[3,8,64,256]{3,2,1,0:T(8,128)} %copy-done.3), kind=kOutput, calls=%fused_computation.73 | convolution fusion | flops 101844736 | bytes 5117952 | tf_op jit(solution)/shard_map/bhqk,bqhd->bkhd/dot_general | solution.py:78
  140.0 3.6 %copy.142 = f32[3,256,1024]{2,1,0:T(8,128)} copy(f32[3,256,1024]{1,2,0:T(8,128)} %bitcast.154) | data formatting | bytes 6291456 | tf_op jit(solution)/shard_map/reshape | solution.py:139
  145.1 1.9 copy.110
  147.1 1.9 copy.112
  149.0 1.2 copy.116
  150.2 1.2 copy.127
  151.4 1.3 copy_bitcast_fusion.2
  153.4 1.7 fusion.68
  156.2 3.3 %fusion.12 = bf16[24,8,8,128]{3,0,2,1:T(8,128)(2,1)} fusion(bf16[24,8,8,128]{3,2,1,0:T(8,128)(2,1)} %get-tuple-element.40, f32[8,8,24]{2,1,0:T(8,128)} %get-tuple-element.33, f32[8,8,24,24]{2,3,1,0:T(8,128)} %copy-done.17), kind=kOutput, calls=%fused_computation.40 | convolution fusion | flops 9745943 | bytes 940032 | tf_op jit(solution)/shard_map/bhqk,qbhd->kbhd/dot_general | solution.py:78
  159.5 1.1 copy.144
  161.5 5.3 %all-to-all-start.7 = ((bf16[24,8,1024]{2,1,0:T(8,128)(2,1)}), bf16[24,8,1024]{2,1,0:T(8,128)(2,1)S(1)}, u32[]{:S(2)}, u32[]{:S(2)}) async-start(bf16[24,8,1024]{2,1,0:T(8,128)(2,1)} %convert_element_type.188), calls=%async_computation.9 | async-start | bytes 786432 | tf_op jit(solution)/shard_map/all_to_all | solution.py:178
  166.8 3.7 %multiply_reduce_fusion = (f32[24,8,8]{0,2,1:T(8,128)}, bf16[24,8,8,128]{3,0,2,1:T(8,128)(2,1)}) fusion(bf16[24,8,8,128]{3,2,1,0:T(8,128)(2,1)} %get-tuple-element.40, bf16[24,8,8,128]{3,2,1,0:T(8,128)(2,1)} %get-tuple-element.41, f32[8,8,24]{2,1,0:T(8,128)} %get-tuple-element.33, f32[8,8,24,24]{2,3,1,0:T(8,128)} %copy-done.17), kind=kOutput, calls=%fused_computation.63 | convolution fusion | flops 10334231 | bytes 1339392 | tf_op jit(solution)/shard_map/bhqk,kbhd->qbhd/dot_general | solution.py:53
  170.5 2.1 fusion.9
  174.2 1.9 convert_element_type.184
  176.1 5.5 %all-to-all-start.6 = ((bf16[24,8,1024]{2,1,0:T(8,128)(2,1)}), bf16[24,8,1024]{2,1,0:T(8,128)(2,1)}, u32[]{:S(2)}, u32[]{:S(2)}) async-start(bf16[24,8,1024]{2,1,0:T(8,128)(2,1)} %convert_element_type.184), calls=%async_computation.7 | async-start | bytes 786432 | tf_op jit(solution)/shard_map/all_to_all | solution.py:177
  181.6 1.8 constant_dynamic-update-slice_fusion.5
  185.6 1.9 convert_element_type.180
  187.6 2.2 all-to-all-done.6
  189.7 4.1 %all-to-all-start.5 = ((bf16[24,8,1024]{2,1,0:T(8,128)(2,1)}), bf16[24,8,1024]{2,1,0:T(8,128)(2,1)}, u32[]{:S(2)}, u32[]{:S(2)}) async-start(bf16[24,8,1024]{2,1,0:T(8,128)(2,1)} %convert_element_type.180), calls=%async_computation.5 | async-start | bytes 786432 | tf_op jit(solution)/shard_map/all_to_all | solution.py:176
  193.9 1.7 constant_dynamic-update-slice_fusion.3
  195.5 1.7 fusion.61
  197.2 8.9 %collective-permute-start.6 = (bf16[5,1,2048]{2,1,0:T(2,128)(2,1)}, bf16[5,1,2048]{2,1,0:T(2,128)(2,1)}, u32[]{:S(2)}, u32[]{:S(2)}) collective-permute-start(bf16[5,1,2048]{2,1,0:T(2,128)(2,1)} %get-tuple-element.4), channel_id=1, source_target_pairs={{1,0},{2,1},{3,2},{5,4},{6,5},{7,6},{9,8},{10,9},{11,10},{13,12},{... | collective-permute-start | bytes 61448 | tf_op jit(solution)/shard_map/ppermute | solution.py:20
  206.1 2.0 collective-permute-start.7
  208.1 1.7 constant_dynamic-update-slice_fusion.2
  209.8 1.8 copy.119
  211.6 1.9 convert_element_type.158
  213.5 5.6 %all-to-all-start.3 = ((bf16[24,8,1024]{2,1,0:T(8,128)(2,1)}), bf16[24,8,1024]{2,1,0:T(8,128)(2,1)}, u32[]{:S(2)}, u32[]{:S(2)}) async-start(bf16[24,8,1024]{2,1,0:T(8,128)(2,1)} %convert_element_type.158), calls=%async_computation.3 | async-start | bytes 786432 | tf_op jit(solution)/shard_map/all_to_all | solution.py:175
  220.1 1.7 constant_dynamic-update-slice_fusion
  221.8 1.7 fusion.62
  223.5 3.3 %collective-permute-start.2 = (bf16[5,1,2048]{2,1,0:T(2,128)(2,1)}, bf16[5,1,2048]{2,1,0:T(2,128)(2,1)}, u32[]{:S(2)}, u32[]{:S(2)}) collective-permute-start(bf16[5,1,2048]{2,1,0:T(2,128)(2,1)} %get-tuple-element.6), channel_id=1, source_target_pairs={{0,1},{1,2},{2,3},{4,5},{5,6},{6,7},{8,9},{9,10},{10,11},{12,13},{... | collective-permute-start | bytes 61448 | tf_op jit(solution)/shard_map/ppermute | solution.py:19
  226.8 2.1 collective-permute-start.3
  230.7 1.8 copy.220
  233.5 1.9 fusion.13
  237.2 4.8 %add_convert_fusion.1 = bf16[3,64,2048]{2,1,0:T(8,128)(2,1)} fusion(bf16[3,64,2048]{2,1,0:T(8,128)(2,1)S(1)} %copy-done.1, bf16[5,64,2048]{2,1,0:T(8,128)(2,1)S(1)} %copy-done.5, bf16[5,1,2048]{2,1,0:T(2,128)(2,1)} %collective-permute-done.3, bf16[5,1,2048]{2,1,0:T(2,128)(2,1)} %collective-permute-done.2, bf16[1,64,2048]{2,1,0:T(8,128)(2,1)} %collective-permute-done.1, ...), kind=kLoop, calls=%fused_computation.13 | loop fusion | flops 22020096 | bytes 4308992 | tf_op jit(solution)/shard_map/convert_element_type | solution.py:183
  241.9 1.2 convert_element_type.181
  244.1 1.2 convert_element_type.185
  245.3 6.1 %add_convert_fusion = bf16[3,64,2048]{2,1,0:T(8,128)(2,1)} fusion(bf16[3,64,2048]{2,1,0:T(8,128)(2,1)S(1)} %copy-done.2, bf16[5,64,2048]{2,1,0:T(8,128)(2,1)} %constant_dynamic-update-slice_fusion.3, bf16[5,1,2048]{2,1,0:T(2,128)(2,1)} %collective-permute-done.7, bf16[5,1,2048]{2,1,0:T(2,128)(2,1)} %collective-permute-done.6, ...), kind=kLoop, calls=%fused_computation.11 | loop fusion | flops 22020096 | bytes 4308992 | tf_op jit(solution)/shard_map/convert_element_type | solution.py:187
  (113 shorter events, 21.4 us)
Async XLA Ops:
  7.2 115.6 %copy-start = (s32[64,3,3]{0,2,1:T(4,128)S(1)}, s32[64,3,3]{0,2,1:T(4,128)}, u32[]{:S(2)}) copy-start(s32[64,3,3]{0,2,1:T(4,128)} %param.13) | copy-start | bytes 6916
  7.2 2.3 copy-start.1
  7.2 25.1 %all-gather.3.cloned.1.call-start = ((), (), s32[]{:S(2)}) async-start(), calls=%async_computation.10 | async-start | bytes 1966080 | tf_op jit(solution)/shard_map/all_gather | solution.py:117
  9.4 1.1 copy-start.29
  9.4 2.2 copy-start.16
  9.4 3.1 %copy-start.2 = (bf16[3,64,2048]{2,1,0:T(8,128)(2,1)S(1)}, bf16[3,64,2048]{2,1,0:T(8,128)(2,1)}, u32[]{:S(2)}) copy-start(bf16[3,64,2048]{2,1,0:T(8,128)(2,1)} %param.10) | copy-start | bytes 2359300
  9.4 44.7 %all-gather.5.cloned.1.call-start = ((), (), s32[]{:S(2)}) async-start(), calls=%async_computation.11 | async-start | bytes 1966080 | tf_op jit(solution)/shard_map/all_gather | solution.py:118
  10.5 231.5 %reduce-scatter.3.cloned.1.call-start = ((), (), s32[]{:S(2)}) async-start(), calls=%async_computation.12 | async-start | bytes 3932160 | tf_op jit(solution)/shard_map/reduce_scatter | solution.py:141
  35.2 1.2 copy-start.3
  65.9 2.4 copy-start.4
  71.8 7.4 %copy-start.7 = (bf16[3,64,1024]{2,1,0:T(8,128)(2,1)S(1)}, bf16[3,64,1024]{2,1,0:T(8,128)(2,1)}, u32[]{:S(2)}) copy-start(bf16[3,64,1024]{2,1,0:T(8,128)(2,1)} %get-tuple-element.19) | copy-start | bytes 1179652
  74.0 19.1 %all-to-all-start = ((bf16[3,64,1024]{2,0,1:T(4,128)(2,1)}), bf16[3,64,1024]{2,0,1:T(4,128)(2,1)}, u32[]{:S(2)}, u32[]{:S(2)}) async-start(bf16[3,64,1024]{2,0,1:T(4,128)(2,1)} %copy.154), calls=%async_computation | async-start | bytes 1048576 | tf_op jit(solution)/shard_map/all_to_all | solution.py:150
  93.1 16.5 %all-to-all-start.1 = ((bf16[3,64,1024]{2,0,1:T(4,128)(2,1)}), bf16[3,64,1024]{2,0,1:T(4,128)(2,1)}, u32[]{:S(2)}, u32[]{:S(2)}) async-start(bf16[3,64,1024]{2,0,1:T(4,128)(2,1)} %copy.155), calls=%async_computation.1 | async-start | bytes 1048576 | tf_op jit(solution)/shard_map/all_to_all | solution.py:151
  98.4 121.7 %collective-permute-start.1 = (bf16[1,64,2048]{2,1,0:T(8,128)(2,1)}, bf16[1,64,2048]{2,1,0:T(8,128)(2,1)}, u32[]{:S(2)}, u32[]{:S(2)}) collective-permute-start(bf16[1,64,2048]{2,1,0:T(8,128)(2,1)} %get-tuple-element.22), channel_id=1, source_target_pairs={{4,0},{8,4},{12,8},{16,12},{20,16},{24,20},{28,24},{5,1},{9,5},{13... | collective-permute-start | bytes 786440 | tf_op jit(solution)/shard_map/ppermute | solution.py:20
  99.7 108.4 %collective-permute-start = (bf16[1,64,2048]{2,1,0:T(8,128)(2,1)}, bf16[1,64,2048]{2,1,0:T(8,128)(2,1)}, u32[]{:S(2)}, u32[]{:S(2)}) collective-permute-start(bf16[1,64,2048]{2,1,0:T(8,128)(2,1)} %get-tuple-element.23), channel_id=1, source_target_pairs={{0,4},{4,8},{8,12},{12,16},{16,20},{20,24},{24,28},{1,5},{5,9},{9,... | collective-permute-start | bytes 786440 | tf_op jit(solution)/shard_map/ppermute | solution.py:19
  104.4 20.8 %copy-start.6 = (bf16[3,64,1024]{2,1,0:T(8,128)(2,1)S(1)}, bf16[3,64,1024]{2,1,0:T(8,128)(2,1)}, u32[]{:S(2)}) copy-start(bf16[3,64,1024]{2,1,0:T(8,128)(2,1)} %get-tuple-element.13) | copy-start | bytes 1179652
  109.6 16.8 %all-to-all-start.2 = ((bf16[3,64,1024]{2,0,1:T(4,128)(2,1)}), bf16[3,64,1024]{2,0,1:T(4,128)(2,1)}, u32[]{:S(2)}, u32[]{:S(2)}) async-start(bf16[3,64,1024]{2,0,1:T(4,128)(2,1)} %copy.156), calls=%async_computation.2 | async-start | bytes 1048576 | tf_op jit(solution)/shard_map/all_to_all | solution.py:152
  116.8 77.1 %collective-permute-start.5 = (bf16[1,64,2048]{2,1,0:T(8,128)(2,1)}, bf16[1,64,2048]{2,1,0:T(8,128)(2,1)}, u32[]{:S(2)}, u32[]{:S(2)}) collective-permute-start(bf16[1,64,2048]{2,1,0:T(8,128)(2,1)} %get-tuple-element.8), channel_id=1, source_target_pairs={{4,0},{8,4},{12,8},{16,12},{20,16},{24,20},{28,24},{5,1},{9,5},{13... | collective-permute-start | bytes 786440 | tf_op jit(solution)/shard_map/ppermute | solution.py:20
  118.0 63.6 %collective-permute-start.4 = (bf16[1,64,2048]{2,1,0:T(8,128)(2,1)}, bf16[1,64,2048]{2,1,0:T(8,128)(2,1)}, u32[]{:S(2)}, u32[]{:S(2)}) collective-permute-start(bf16[1,64,2048]{2,1,0:T(8,128)(2,1)} %get-tuple-element.9), channel_id=1, source_target_pairs={{0,4},{4,8},{8,12},{12,16},{16,20},{20,24},{24,28},{1,5},{5,9},{9,... | collective-permute-start | bytes 786440 | tf_op jit(solution)/shard_map/ppermute | solution.py:19
  126.4 23.8 %all-to-all-start.4 = ((bf16[3,64,1024]{2,0,1:T(4,128)(2,1)}), bf16[3,64,1024]{2,0,1:T(4,128)(2,1)}, u32[]{:S(2)}, u32[]{:S(2)}) async-start(bf16[3,64,1024]{2,0,1:T(4,128)(2,1)} %copy.157), calls=%async_computation.4 | async-start | bytes 1048576 | tf_op jit(solution)/shard_map/all_to_all | solution.py:153
  133.0 111.0 %reduce-scatter.5.cloned.1.call-start = ((), (), s32[]{:S(2)}) async-start(), calls=%async_computation.13 | async-start | bytes 3932160 | tf_op jit(solution)/shard_map/reduce_scatter | solution.py:142
  143.6 0.8 copy-start.19
  150.2 2.5 copy-start.28
  152.7 2.4 copy-start.10
  152.8 2.4 copy-start.12
  153.4 2.8 %copy-start.17 = (f32[8,8,24,24]{2,3,1,0:T(8,128)}, f32[8,8,24,24]{2,3,1,0:T(8,128)S(1)}, u32[]{:S(2)}) copy-start(f32[8,8,24,24]{2,3,1,0:T(8,128)S(1)} %fusion.6) | copy-start | bytes 442372
  161.5 14.6 %all-to-all-start.7 = ((bf16[24,8,1024]{2,1,0:T(8,128)(2,1)}), bf16[24,8,1024]{2,1,0:T(8,128)(2,1)S(1)}, u32[]{:S(2)}, u32[]{:S(2)}) async-start(bf16[24,8,1024]{2,1,0:T(8,128)(2,1)} %convert_element_type.188), calls=%async_computation.9 | async-start | bytes 786432 | tf_op jit(solution)/shard_map/all_to_all | solution.py:178
  170.5 2.1 copy-start.13
  172.6 0.7 copy-start.14
  176.1 13.6 %all-to-all-start.6 = ((bf16[24,8,1024]{2,1,0:T(8,128)(2,1)}), bf16[24,8,1024]{2,1,0:T(8,128)(2,1)}, u32[]{:S(2)}, u32[]{:S(2)}) async-start(bf16[24,8,1024]{2,1,0:T(8,128)(2,1)} %convert_element_type.184), calls=%async_computation.7 | async-start | bytes 786432 | tf_op jit(solution)/shard_map/all_to_all | solution.py:177
  181.6 2.8 %copy-start.11 = (bf16[24,8,8,128]{3,2,1,0:T(8,128)(2,1)S(1)}, bf16[24,8,8,128]{3,2,1,0:T(8,128)(2,1)}, u32[]{:S(2)}) copy-start(bf16[24,8,8,128]{3,2,1,0:T(8,128)(2,1)} %copy-done.10) | copy-start | bytes 1179652
  181.6 2.8 %copy-start.15 = (bf16[8,8,24,24]{2,3,1,0:T(8,128)(2,1)S(1)}, bf16[8,8,24,24]{2,3,1,0:T(8,128)(2,1)}, u32[]{:S(2)}) copy-start(bf16[8,8,24,24]{2,3,1,0:T(8,128)(2,1)} %copy-done.14) | copy-start | bytes 221188
  189.7 23.8 %all-to-all-start.5 = ((bf16[24,8,1024]{2,1,0:T(8,128)(2,1)}), bf16[24,8,1024]{2,1,0:T(8,128)(2,1)}, u32[]{:S(2)}, u32[]{:S(2)}) async-start(bf16[24,8,1024]{2,1,0:T(8,128)(2,1)} %convert_element_type.180), calls=%async_computation.5 | async-start | bytes 786432 | tf_op jit(solution)/shard_map/all_to_all | solution.py:176
  197.2 48.1 %collective-permute-start.6 = (bf16[5,1,2048]{2,1,0:T(2,128)(2,1)}, bf16[5,1,2048]{2,1,0:T(2,128)(2,1)}, u32[]{:S(2)}, u32[]{:S(2)}) collective-permute-start(bf16[5,1,2048]{2,1,0:T(2,128)(2,1)} %get-tuple-element.4), channel_id=1, source_target_pairs={{1,0},{2,1},{3,2},{5,4},{6,5},{7,6},{9,8},{10,9},{11,10},{13,12},{... | collective-permute-start | bytes 61448 | tf_op jit(solution)/shard_map/ppermute | solution.py:20
  206.1 39.2 %collective-permute-start.7 = (bf16[5,1,2048]{2,1,0:T(2,128)(2,1)}, bf16[5,1,2048]{2,1,0:T(2,128)(2,1)}, u32[]{:S(2)}, u32[]{:S(2)}) collective-permute-start(bf16[5,1,2048]{2,1,0:T(2,128)(2,1)} %get-tuple-element.5), channel_id=1, source_target_pairs={{0,1},{1,2},{2,3},{4,5},{5,6},{6,7},{8,9},{9,10},{10,11},{12,13},{... | collective-permute-start | bytes 61448 | tf_op jit(solution)/shard_map/ppermute | solution.py:19
  213.5 18.9 %all-to-all-start.3 = ((bf16[24,8,1024]{2,1,0:T(8,128)(2,1)}), bf16[24,8,1024]{2,1,0:T(8,128)(2,1)}, u32[]{:S(2)}, u32[]{:S(2)}) async-start(bf16[24,8,1024]{2,1,0:T(8,128)(2,1)} %convert_element_type.158), calls=%async_computation.3 | async-start | bytes 786432 | tf_op jit(solution)/shard_map/all_to_all | solution.py:175
  223.5 13.2 %collective-permute-start.2 = (bf16[5,1,2048]{2,1,0:T(2,128)(2,1)}, bf16[5,1,2048]{2,1,0:T(2,128)(2,1)}, u32[]{:S(2)}, u32[]{:S(2)}) collective-permute-start(bf16[5,1,2048]{2,1,0:T(2,128)(2,1)} %get-tuple-element.6), channel_id=1, source_target_pairs={{0,1},{1,2},{2,3},{4,5},{5,6},{6,7},{8,9},{9,10},{10,11},{12,13},{... | collective-permute-start | bytes 61448 | tf_op jit(solution)/shard_map/ppermute | solution.py:19
  226.8 9.9 %collective-permute-start.3 = (bf16[5,1,2048]{2,1,0:T(2,128)(2,1)}, bf16[5,1,2048]{2,1,0:T(2,128)(2,1)}, u32[]{:S(2)}, u32[]{:S(2)}) collective-permute-start(bf16[5,1,2048]{2,1,0:T(2,128)(2,1)} %get-tuple-element.7), channel_id=1, source_target_pairs={{1,0},{2,1},{3,2},{5,4},{6,5},{7,6},{9,8},{10,9},{11,10},{13,12},{... | collective-permute-start | bytes 61448 | tf_op jit(solution)/shard_map/ppermute | solution.py:20
  233.5 2.1 copy-start.9
  235.4 1.2 copy-start.18
  235.4 1.7 copy-start.5
  235.4 1.7 copy-start.20
  235.4 1.7 copy-start.21
  235.4 1.7 copy-start.22
  235.4 1.7 copy-start.23
  235.4 1.7 copy-start.24
  235.4 1.7 copy-start.25
  235.5 1.7 copy-start.26
  235.5 1.7 copy-start.27
  243.1 2.2 copy-start.8
Sparse Core Ops, SparseCore 0:
  10.2 22.1 all-gather.2
  34.5 19.6 all-gather.4
  71.9 37.5 reduce-scatter.2
  143.8 42.4 reduce-scatter.4
where the time goes:
time: 260 us; the launch traced here: 258 us
  starting transfers between devices  71.8 us (28%)
  local copies, waits for them, and re-layouts  66.4 us (26%)
  waiting for transfers between devices  52.5 us (20%)
  matrix products  33.9 us (13%)
  other arithmetic  18.9 us (7%)
  between operations  14.3 us (6%)
    all_gather x1, waiting for transfers between devices, body(): lax.all_gather(key[:, :, :half_width], 'cols', axis=1, tiled=True)  18.9 us
    unnamed x70, local copies, waits for them, and re-layouts  16.6 us
    all_gather x1, waiting for transfers between devices, body(): lax.all_gather(value[:, :, :half_width], 'cols', axis=1, tiled=True)  15.7 us
    ppermute x4, starting transfers between devices, padded(): before = lax.ppermute(last, axis, up)  14.7 us
    ppermute x4, starting transfers between devices, padded(): after = lax.ppermute(leading, axis, down)  13.6 us
    all_to_all x1, waiting for transfers between devices, body(): lax.all_to_all(query[:, :, half_width:], 'rows', split_axis=1, concat_axi...  12.7 us
    convert_element_type x8, local copies, waits for them, and re-layouts, body(): piece.reshape(column_flat).astype(jnp.bfloat16)  11.3 us
    dot_general x2, matrix products, line_attention(): jnp.einsum('bhqk,' + key_layout_shape + '->' + query_form, rounded, value...  10.4 us
  transfers between devices with their start and end apart: 20, of which 5 were waited for; matrix products, arithmetic and copies ran while one was open for 35% of the time, Pallas kernels for 0%

commit v1 on v0

--- a/solution.py
+++ b/solution.py
@@ -1,12 +1,42 @@
+import functools
 import math
 import jax
 import jax.numpy as jnp
 from jax import lax
 from jax.sharding import PartitionSpec as P
+from jax.lax import axis_index, ppermute, psum
 
 HEAD_DIM = 128
 SHEET_ROW_BLOCKS = 2
 COL_BLOCKS = 3
+
+
+def push_the_windows(chunk, out_dim, inp):
+    r1 = chunk.shape
+    opened = chunk.reshape(*r1[:out_dim], inp, r1[out_dim] // inp, *r1[out_dim + 1 :])
+    return jnp.moveaxis(opened, out_dim, 0)
+
+
+def define_the_frame(panel, dim_i):
+    fresh = list(panel.shape[1:])
+    fresh[dim_i] *= panel.shape[0]
+    return jnp.moveaxis(panel, 0, dim_i).reshape(fresh)
+
+
+def list_the_steps_all(tile_in, comm_axis, target, xin):
+    heard, tile_out = (psum(1, comm_axis), axis_index(comm_axis))
+    arr_next = push_the_windows(tile_in, target, heard)
+    ledger = [arr_next[tile_out]]
+    p = 1
+    while p < heard:
+        piece_out = arr_next[tile_out ^ p]
+        ledger.append(ppermute(piece_out, comm_axis, [(k0, k0 ^ p) for k0 in range(heard)]))
+        p = p + 1
+    arr_next = jnp.stack(ledger, axis=0)[tile_out ^ jnp.arange(heard)]
+    return define_the_frame(arr_next, xin)
+
+
+_wrap_pools = functools.partial(list_the_steps_all, comm_axis="rows", target=0, xin=1)
 
 
 def padded(array, sides, width):
@@ -175,7 +205,7 @@
         lax.all_to_all(col_pieces[0], "rows", split_axis=0, concat_axis=1, tiled=True),
         lax.all_to_all(col_pieces[1], "rows", split_axis=0, concat_axis=1, tiled=True),
         lax.all_to_all(col_pieces[2], "rows", split_axis=0, concat_axis=1, tiled=True),
-        lax.all_to_all(col_pieces[3], "rows", split_axis=0, concat_axis=1, tiled=True),
+        _wrap_pools(col_pieces[3]),
     )
     lepe = depthwise(padded_value, taps, rows_here, cols_here, False)
     back_conv = depthwise(padded_grad, taps, rows_here, cols_here, True)

time: 260 us -> 290 us (1.12)
  the two profiles are of different devices: /device:TPU:1 before, /device:TPU:0 now
where the time goes in v1:
time: 290 us; the launch traced here: 287 us
  local copies, waits for them, and re-layouts  77.5 us (27%)
  starting transfers between devices  72.5 us (25%)
  waiting for transfers between devices  66.9 us (23%)
  matrix products  35.1 us (12%)
  other arithmetic  20.9 us (7%)
  between operations  14.4 us (5%)
    unnamed x74, local copies, waits for them, and re-layouts  20.8 us
    all_gather x1, waiting for transfers between devices, body(): lax.all_gather(key[:, :, :half_width], 'cols', axis=1, tiled=True)  19.1 us
    ppermute x7, starting transfers between devices, list_the_steps_all(): ppermute(piece_out, comm_axis, [(k0, k0 ^ p) for k0 in range(heard)])  18.9 us
    ppermute x4, starting transfers between devices, padded(): before = lax.ppermute(last, axis, up)  16.3 us
    all_gather x1, waiting for transfers between devices, body(): lax.all_gather(value[:, :, :half_width], 'cols', axis=1, tiled=True)  15.7 us
    ppermute x7, waiting for transfers between devices, list_the_steps_all(): ppermute(piece_out, comm_axis, [(k0, k0 ^ p) for k0 in range(heard)])  11.7 us
    convert_element_type x8, local copies, waits for them, and re-layouts, body(): piece.reshape(column_flat).astype(jnp.bfloat16)  11.2 us
    dot_general x2, matrix products, line_attention(): jnp.einsum('bhqk,' + key_layout_shape + '->' + query_form, rounded, value...  10.7 us
  transfers between devices with their start and end apart: 26, of which 10 were waited for; matrix products, arithmetic and copies ran while one was open for 37% of the time, Pallas kernels for 0%

profile of v1, /device:TPU:0, one launch (start us, length us, event | category | flops | bytes accessed | tf_op | source)
XLA Modules:
  0.0 287.3 jit_solution(10318075948981922956)
XLA Ops:
  7.2 2.1 fusion.65
  13.4 19.1 %all-gather.3.cloned.1.call-done = bf16[3,256,1024]{2,1,0:T(8,128)(2,1)} async-done(((bf16[3,64,1024]{2,1,0:T(8,128)(2,1)}), bf16[3,256,1024]{2,1,0:T(8,128)(2,1)}) %all-gather.3.cloned.1.call-update) | async-done | bytes 1572880 | tf_op jit(solution)/shard_map/all_gather | solution.py:147
  32.6 1.7 copy.99
  36.6 2.0 fusion.70
  38.7 15.7 %all-gather.5.cloned.1.call-done = bf16[3,256,1024]{2,1,0:T(8,128)(2,1)} async-done(((bf16[3,64,1024]{2,1,0:T(8,128)(2,1)}), bf16[3,256,1024]{2,1,0:T(8,128)(2,1)}) %all-gather.5.cloned.1.call-update) | async-done | bytes 1572880 | tf_op jit(solution)/shard_map/all_gather | solution.py:148
  54.4 2.6 copy.102
  57.0 6.8 %multiply_reduce_fusion.1 = (f32[3,64,8]{1,2,0:T(8,128)}, bf16[3,8,8,8,128]{4,3,2,1,0:T(8,128)(2,1)}) fusion(bf16[3,8,8,8,128]{4,3,2,1,0:T(8,128)(2,1)} %get-tuple-element.12, bf16[3,256,8,128]{1,3,2,0:T(8,128)(2,1)} %bitcast.184, f32[3,8,64]{2,1,0:T(8,128)} %get-tuple-element.44, f32[3,8,64,256]{3,2,1,0:T(8,128)} %copy-done.3), kind=kOutput, calls=%fused_computation.65 | convolution fusion | flops 102629632 | bytes 3944448 | tf_op jit(solution)/shard_map/bhqk,bkhd->bqhd/dot_general | solution.py:83
  63.7 2.5 multiply_convert_fusion
  66.2 2.4 fusion.26
  68.6 3.5 %copy.136 = f32[3,256,1024]{2,1,0:T(8,128)} copy(f32[3,256,1024]{1,2,0:T(8,128)} %bitcast.182) | data formatting | bytes 6291456 | tf_op jit(solution)/shard_map/reshape | solution.py:168
  74.3 5.4 %collective-permute-start = (bf16[1,64,2048]{2,1,0:T(8,128)(2,1)}, bf16[1,64,2048]{2,1,0:T(8,128)(2,1)}, u32[]{:S(2)}, u32[]{:S(2)}) collective-permute-start(bf16[1,64,2048]{2,1,0:T(8,128)(2,1)} %get-tuple-element.23), channel_id=1, source_target_pairs={{0,4},{4,8},{8,12},{12,16},{16,20},{20,24},{24,28},{1,5},{5,9},{9,... | collective-permute-start | bytes 786440 | tf_op jit(solution)/shard_map/ppermute | solution.py:49
  81.9 5.2 %collective-permute-start.11 = (bf16[1,64,2048]{2,1,0:T(8,128)(2,1)}, bf16[1,64,2048]{2,1,0:T(8,128)(2,1)}, u32[]{:S(2)}, u32[]{:S(2)}) collective-permute-start(bf16[1,64,2048]{2,1,0:T(8,128)(2,1)} %get-tuple-element.9), channel_id=1, source_target_pairs={{0,4},{4,8},{8,12},{12,16},{16,20},{20,24},{24,28},{1,5},{5,9},{9,... | collective-permute-start | bytes 786440 | tf_op jit(solution)/shard_map/ppermute | solution.py:49
  88.3 5.0 %all-to-all-start = ((bf16[3,64,1024]{2,0,1:T(4,128)(2,1)}), bf16[3,64,1024]{2,0,1:T(4,128)(2,1)}, u32[]{:S(2)}, u32[]{:S(2)}) async-start(bf16[3,64,1024]{2,0,1:T(4,128)(2,1)} %copy.153), calls=%async_computation | async-start | bytes 1048576 | tf_op jit(solution)/shard_map/all_to_all | solution.py:180
  93.4 1.7 fusion.68
  98.7 2.1 copy.155
  102.6 4.7 %all-to-all-done = bf16[3,64,1024]{2,0,1:T(4,128)(2,1)} async-done(((bf16[3,64,1024]{2,0,1:T(4,128)(2,1)}), bf16[3,64,1024]{2,0,1:T(4,128)(2,1)}, u32[]{:S(2)}, u32[]{:S(2)}) %all-to-all-start) | async-done | bytes 393248 | tf_op jit(solution)/shard_map/all_to_all | solution.py:180
  107.2 4.4 %all-to-all-start.1 = ((bf16[3,64,1024]{2,0,1:T(4,128)(2,1)}), bf16[3,64,1024]{2,0,1:T(4,128)(2,1)}, u32[]{:S(2)}, u32[]{:S(2)}) async-start(bf16[3,64,1024]{2,0,1:T(4,128)(2,1)} %copy.154), calls=%async_computation.1 | async-start | bytes 1048576 | tf_op jit(solution)/shard_map/all_to_all | solution.py:181
  111.7 1.7 constant_dynamic-update-slice_fusion.5
  114.3 1.7 constant_dynamic-update-slice_fusion.3
  116.0 10.4 %all-to-all-done.1 = bf16[3,64,1024]{2,0,1:T(4,128)(2,1)} async-done(((bf16[3,64,1024]{2,0,1:T(4,128)(2,1)}), bf16[3,64,1024]{2,0,1:T(4,128)(2,1)}, u32[]{:S(2)}, u32[]{:S(2)}) %all-to-all-start.1) | async-done | bytes 393248 | tf_op jit(solution)/shard_map/all_to_all | solution.py:181
  126.4 4.1 %all-to-all-start.2 = ((bf16[3,64,1024]{2,0,1:T(4,128)(2,1)}), bf16[3,64,1024]{2,0,1:T(4,128)(2,1)}, u32[]{:S(2)}, u32[]{:S(2)}) async-start(bf16[3,64,1024]{2,0,1:T(4,128)(2,1)} %copy.155), calls=%async_computation.2 | async-start | bytes 1048576 | tf_op jit(solution)/shard_map/all_to_all | solution.py:182
  130.6 1.7 fusion.62
  133.6 3.8 %collective-permute-start.14 = (bf16[5,1,2048]{2,1,0:T(2,128)(2,1)}, bf16[5,1,2048]{2,1,0:T(2,128)(2,1)}, u32[]{:S(2)}, u32[]{:S(2)}) collective-permute-start(bf16[5,1,2048]{2,1,0:T(2,128)(2,1)} %get-tuple-element.5), channel_id=1, source_target_pairs={{0,1},{1,2},{2,3},{4,5},{5,6},{6,7},{8,9},{9,10},{10,11},{12,13},{... | collective-permute-start | bytes 61448 | tf_op jit(solution)/shard_map/ppermute | solution.py:49
  137.3 1.7 constant_dynamic-update-slice_fusion.2
  140.0 4.8 %all-to-all-done.2 = bf16[3,64,1024]{2,0,1:T(4,128)(2,1)} async-done(((bf16[3,64,1024]{2,0,1:T(4,128)(2,1)}), bf16[3,64,1024]{2,0,1:T(4,128)(2,1)}, u32[]{:S(2)}, u32[]{:S(2)}) %all-to-all-start.2) | async-done | bytes 393248 | tf_op jit(solution)/shard_map/all_to_all | solution.py:182
  144.9 4.1 %all-to-all-start.4 = ((bf16[3,64,1024]{2,0,1:T(4,128)(2,1)}), bf16[3,64,1024]{2,0,1:T(4,128)(2,1)}, u32[]{:S(2)}, u32[]{:S(2)}) async-start(bf16[3,64,1024]{2,0,1:T(4,128)(2,1)} %copy.156), calls=%async_computation.4 | async-start | bytes 1048576 | tf_op jit(solution)/shard_map/all_to_all | solution.py:183
  149.1 6.7 %fusion.23 = f32[3,8,256,128]{2,3,1,0:T(8,128)} fusion(bf16[3,8,8,8,128]{4,3,2,1,0:T(8,128)(2,1)S(1)} %copy-done.17, f32[3,8,64]{2,1,0:T(8,128)} %get-tuple-element.44, f32[3,8,64,256]{3,2,1,0:T(8,128)} %copy-done.3), kind=kOutput, calls=%fused_computation.74 | convolution fusion | flops 101844736 | bytes 5117952 | tf_op jit(solution)/shard_map/bhqk,bqhd->bkhd/dot_general | solution.py:108
  155.8 3.5 %copy.141 = f32[3,256,1024]{2,1,0:T(8,128)} copy(f32[3,256,1024]{1,2,0:T(8,128)} %bitcast.183) | data formatting | bytes 6291456 | tf_op jit(solution)/shard_map/reshape | solution.py:169
  159.4 1.7 constant_dynamic-update-slice_fusion
  161.0 1.7 fusion.63
  162.7 1.9 collective-permute-start.2
  164.6 1.5 collective-permute-start.3
  166.1 2.0 copy.109
  168.1 2.1 copy.111
  174.6 1.7 fusion.69
  177.4 3.9 %multiply_reduce_fusion = (f32[24,8,8]{0,2,1:T(8,128)}, bf16[24,8,8,128]{3,0,2,1:T(8,128)(2,1)}) fusion(bf16[24,8,8,128]{3,2,1,0:T(8,128)(2,1)} %get-tuple-element.48, bf16[24,8,8,128]{3,2,1,0:T(8,128)(2,1)} %get-tuple-element.49, f32[8,8,24]{2,1,0:T(8,128)} %get-tuple-element.41, f32[8,8,24,24]{2,3,1,0:T(8,128)} %copy-done.15), kind=kOutput, calls=%fused_computation.64 | convolution fusion | flops 10334231 | bytes 1339392 | tf_op jit(solution)/shard_map/bhqk,kbhd->qbhd/dot_general | solution.py:83
  181.3 2.1 fusion.9
  185.7 5.9 %all-to-all-start.6 = ((bf16[24,8,1024]{2,1,0:T(8,128)(2,1)}), bf16[24,8,1024]{2,1,0:T(8,128)(2,1)S(1)}, u32[]{:S(2)}, u32[]{:S(2)}) async-start(bf16[24,8,1024]{2,1,0:T(8,128)(2,1)} %convert_element_type.185), calls=%async_computation.7 | async-start | bytes 786432 | tf_op jit(solution)/shard_map/all_to_all | solution.py:207
  191.6 3.1 %fusion.12 = bf16[24,8,8,128]{3,0,2,1:T(8,128)(2,1)} fusion(bf16[24,8,8,128]{3,2,1,0:T(8,128)(2,1)} %get-tuple-element.48, f32[8,8,24]{2,1,0:T(8,128)} %get-tuple-element.41, f32[8,8,24,24]{2,3,1,0:T(8,128)} %copy-done.15), kind=kOutput, calls=%fused_computation.41 | convolution fusion | flops 9745943 | bytes 940032 | tf_op jit(solution)/shard_map/bhqk,qbhd->kbhd/dot_general | solution.py:108
  194.6 1.8 copy.143
  196.5 1.9 convert_element_type.189
  198.4 1.7 dynamic-slice_bitcast_fusion
  200.1 2.0 collective-permute-start.4
  202.1 1.6 fusion.10
  204.5 1.9 convert_element_type.181
  206.4 1.8 copy.118
  208.3 1.9 convert_element_type.159
  210.2 1.5 collective-permute-start.5
  213.1 4.1 %all-to-all-start.5 = ((bf16[24,8,1024]{2,1,0:T(8,128)(2,1)}), bf16[24,8,1024]{2,1,0:T(8,128)(2,1)}, u32[]{:S(2)}, u32[]{:S(2)}) async-start(bf16[24,8,1024]{2,1,0:T(8,128)(2,1)} %convert_element_type.181), calls=%async_computation.5 | async-start | bytes 786432 | tf_op jit(solution)/shard_map/all_to_all | solution.py:206
  217.2 2.8 collective-permute-start.6
  221.4 4.1 %collective-permute-done.6 = bf16[3,8,1024]{2,1,0:T(8,128)(2,1)S(1)} collective-permute-done((bf16[3,8,1024]{2,1,0:T(8,128)(2,1)}, bf16[3,8,1024]{2,1,0:T(8,128)(2,1)S(1)}, u32[]{:S(2)}, u32[]{:S(2)}) %collective-permute-start.6) | collective-permute-done | bytes 49184 | tf_op jit(solution)/shard_map/ppermute | solution.py:33
  225.5 5.0 %collective-permute-start.7 = (bf16[3,8,1024]{2,1,0:T(8,128)(2,1)}, bf16[3,8,1024]{2,1,0:T(8,128)(2,1)S(1)}, u32[]{:S(2)}, u32[]{:S(2)}) collective-permute-start(bf16[3,8,1024]{2,1,0:T(8,128)(2,1)} %get-tuple-element.27), channel_id=1, source_target_pairs={{0,16},{4,20},{8,24},{12,28},{16,0},{20,4},{24,8},{28,12},{1,17},{... | collective-permute-start | bytes 147464 | tf_op jit(solution)/shard_map/ppermute | solution.py:33
  231.2 1.7 collective-permute-done.7
  232.8 2.9 %collective-permute-start.8 = (bf16[3,8,1024]{2,1,0:T(8,128)(2,1)}, bf16[3,8,1024]{2,1,0:T(8,128)(2,1)S(1)}, u32[]{:S(2)}, u32[]{:S(2)}) collective-permute-start(bf16[3,8,1024]{2,1,0:T(8,128)(2,1)} %get-tuple-element.26), channel_id=1, source_target_pairs={{0,20},{4,16},{8,28},{12,24},{16,4},{20,0},{24,12},{28,8},{1,21},{... | collective-permute-start | bytes 147464 | tf_op jit(solution)/shard_map/ppermute | solution.py:33
  236.4 2.6 collective-permute-done.8
  238.9 2.4 collective-permute-start.9
  241.9 3.3 %collective-permute-done.9 = bf16[3,8,1024]{2,1,0:T(8,128)(2,1)} collective-permute-done((bf16[3,8,1024]{2,1,0:T(8,128)(2,1)}, bf16[3,8,1024]{2,1,0:T(8,128)(2,1)}, u32[]{:S(2)}, u32[]{:S(2)}) %collective-permute-start.9) | collective-permute-done | bytes 49184 | tf_op jit(solution)/shard_map/ppermute | solution.py:33
  245.2 2.3 collective-permute-start.10
  247.5 4.1 %all-to-all-start.3 = ((bf16[24,8,1024]{2,1,0:T(8,128)(2,1)}), bf16[24,8,1024]{2,1,0:T(8,128)(2,1)}, u32[]{:S(2)}, u32[]{:S(2)}) async-start(bf16[24,8,1024]{2,1,0:T(8,128)(2,1)} %convert_element_type.159), calls=%async_computation.3 | async-start | bytes 786432 | tf_op jit(solution)/shard_map/all_to_all | solution.py:205
  254.5 2.4 gather_fusion
  256.9 1.8 copy_bitcast_fusion.6
  261.9 1.8 fusion.13
  265.1 6.2 %add_convert_fusion.1 = bf16[3,64,2048]{2,1,0:T(8,128)(2,1)} fusion(bf16[3,64,2048]{2,1,0:T(8,128)(2,1)S(1)} %copy-done.1, bf16[5,64,2048]{2,1,0:T(8,128)(2,1)} %constant_dynamic-update-slice_fusion, bf16[5,1,2048]{2,1,0:T(2,128)(2,1)} %collective-permute-done.3, bf16[5,1,2048]{2,1,0:T(2,128)(2,1)} %collective-permute-done.2, ...), kind=kLoop, calls=%fused_computation.14 | loop fusion | flops 22020096 | bytes 4308992 | tf_op jit(solution)/shard_map/convert_element_type | solution.py:213
  274.6 6.1 %add_convert_fusion = bf16[3,64,2048]{2,1,0:T(8,128)(2,1)} fusion(bf16[3,64,2048]{2,1,0:T(8,128)(2,1)S(1)} %copy-done.2, bf16[5,64,2048]{2,1,0:T(8,128)(2,1)} %constant_dynamic-update-slice_fusion.3, bf16[5,1,2048]{2,1,0:T(2,128)(2,1)} %collective-permute-done.14, bf16[5,1,2048]{2,1,0:T(2,128)(2,1)} %collective-permute-done.13, ...), kind=kLoop, calls=%fused_computation.12 | loop fusion | flops 22020096 | bytes 4308992 | tf_op jit(solution)/shard_map/convert_element_type | solution.py:217
  (134 shorter events, 44.4 us)
Async XLA Ops:
  7.2 86.1 %copy-start = (s32[64,3,3]{0,2,1:T(4,128)S(1)}, s32[64,3,3]{0,2,1:T(4,128)}, u32[]{:S(2)}) copy-start(s32[64,3,3]{0,2,1:T(4,128)} %param.13) | copy-start | bytes 6916
  7.2 2.3 copy-start.1
  7.2 25.4 %all-gather.3.cloned.1.call-start = ((), (), s32[]{:S(2)}) async-start(), calls=%async_computation.9 | async-start | bytes 1966080 | tf_op jit(solution)/shard_map/all_gather | solution.py:147
  9.4 1.1 copy-start.28
  9.4 2.3 copy-start.14
  9.4 3.1 %copy-start.2 = (bf16[3,64,2048]{2,1,0:T(8,128)(2,1)S(1)}, bf16[3,64,2048]{2,1,0:T(8,128)(2,1)}, u32[]{:S(2)}) copy-start(bf16[3,64,2048]{2,1,0:T(8,128)(2,1)} %param.10) | copy-start | bytes 2359300
  9.4 45.0 %all-gather.5.cloned.1.call-start = ((), (), s32[]{:S(2)}) async-start(), calls=%async_computation.10 | async-start | bytes 1966080 | tf_op jit(solution)/shard_map/all_gather | solution.py:148
  10.5 260.8 %reduce-scatter.3.cloned.1.call-start = ((), (), s32[]{:S(2)}) async-start(), calls=%async_computation.11 | async-start | bytes 3932160 | tf_op jit(solution)/shard_map/reduce_scatter | solution.py:171
  35.5 1.2 copy-start.3
  66.2 2.4 copy-start.4
  72.2 15.0 %copy-start.8 = (bf16[3,64,1024]{2,1,0:T(8,128)(2,1)S(1)}, bf16[3,64,1024]{2,1,0:T(8,128)(2,1)}, u32[]{:S(2)}) copy-start(bf16[3,64,1024]{2,1,0:T(8,128)(2,1)} %get-tuple-element.17) | copy-start | bytes 1179652
  73.0 86.3 %collective-permute-start.1 = (bf16[1,64,2048]{2,1,0:T(8,128)(2,1)}, bf16[1,64,2048]{2,1,0:T(8,128)(2,1)}, u32[]{:S(2)}, u32[]{:S(2)}) collective-permute-start(bf16[1,64,2048]{2,1,0:T(8,128)(2,1)} %get-tuple-element.22), channel_id=1, source_target_pairs={{4,0},{8,4},{12,8},{16,12},{20,16},{24,20},{28,24},{5,1},{9,5},{13... | collective-permute-start | bytes 786440 | tf_op jit(solution)/shard_map/ppermute | solution.py:50
  74.3 23.2 %copy-start.5 = (bf16[3,64,1024]{2,1,0:T(8,128)(2,1)S(1)}, bf16[3,64,1024]{2,1,0:T(8,128)(2,1)}, u32[]{:S(2)}) copy-start(bf16[3,64,1024]{2,1,0:T(8,128)(2,1)} %get-tuple-element.19) | copy-start | bytes 1179652
  74.3 63.0 %collective-permute-start = (bf16[1,64,2048]{2,1,0:T(8,128)(2,1)}, bf16[1,64,2048]{2,1,0:T(8,128)(2,1)}, u32[]{:S(2)}, u32[]{:S(2)}) collective-permute-start(bf16[1,64,2048]{2,1,0:T(8,128)(2,1)} %get-tuple-element.23), channel_id=1, source_target_pairs={{0,4},{4,8},{8,12},{12,16},{16,20},{20,24},{24,28},{1,5},{5,9},{9,... | collective-permute-start | bytes 786440 | tf_op jit(solution)/shard_map/ppermute | solution.py:49
  80.6 33.7 %collective-permute-start.12 = (bf16[1,64,2048]{2,1,0:T(8,128)(2,1)}, bf16[1,64,2048]{2,1,0:T(8,128)(2,1)}, u32[]{:S(2)}, u32[]{:S(2)}) collective-permute-start(bf16[1,64,2048]{2,1,0:T(8,128)(2,1)} %get-tuple-element.8), channel_id=1, source_target_pairs={{4,0},{8,4},{12,8},{16,12},{20,16},{24,20},{28,24},{5,1},{9,5},{13... | collective-permute-start | bytes 786440 | tf_op jit(solution)/shard_map/ppermute | solution.py:50
  81.9 29.7 %collective-permute-start.11 = (bf16[1,64,2048]{2,1,0:T(8,128)(2,1)}, bf16[1,64,2048]{2,1,0:T(8,128)(2,1)}, u32[]{:S(2)}, u32[]{:S(2)}) collective-permute-start(bf16[1,64,2048]{2,1,0:T(8,128)(2,1)} %get-tuple-element.9), channel_id=1, source_target_pairs={{0,4},{4,8},{8,12},{12,16},{16,20},{20,24},{24,28},{1,5},{5,9},{9,... | collective-permute-start | bytes 786440 | tf_op jit(solution)/shard_map/ppermute | solution.py:49
  88.3 18.9 %all-to-all-start = ((bf16[3,64,1024]{2,0,1:T(4,128)(2,1)}), bf16[3,64,1024]{2,0,1:T(4,128)(2,1)}, u32[]{:S(2)}, u32[]{:S(2)}) async-start(bf16[3,64,1024]{2,0,1:T(4,128)(2,1)} %copy.153), calls=%async_computation | async-start | bytes 1048576 | tf_op jit(solution)/shard_map/all_to_all | solution.py:180
  97.6 3.3 %copy-start.6 = (bf16[3,64,1024]{2,1,0:T(8,128)(2,1)S(1)}, bf16[3,64,1024]{2,1,0:T(8,128)(2,1)}, u32[]{:S(2)}) copy-start(bf16[3,64,1024]{2,1,0:T(8,128)(2,1)} %get-tuple-element.13) | copy-start | bytes 1179652
  107.2 19.2 %all-to-all-start.1 = ((bf16[3,64,1024]{2,0,1:T(4,128)(2,1)}), bf16[3,64,1024]{2,0,1:T(4,128)(2,1)}, u32[]{:S(2)}, u32[]{:S(2)}) async-start(bf16[3,64,1024]{2,0,1:T(4,128)(2,1)} %copy.154), calls=%async_computation.1 | async-start | bytes 1048576 | tf_op jit(solution)/shard_map/all_to_all | solution.py:181
  126.4 18.4 %all-to-all-start.2 = ((bf16[3,64,1024]{2,0,1:T(4,128)(2,1)}), bf16[3,64,1024]{2,0,1:T(4,128)(2,1)}, u32[]{:S(2)}, u32[]{:S(2)}) async-start(bf16[3,64,1024]{2,0,1:T(4,128)(2,1)} %copy.155), calls=%async_computation.2 | async-start | bytes 1048576 | tf_op jit(solution)/shard_map/all_to_all | solution.py:182
  132.3 142.4 %collective-permute-start.13 = (bf16[5,1,2048]{2,1,0:T(2,128)(2,1)}, bf16[5,1,2048]{2,1,0:T(2,128)(2,1)}, u32[]{:S(2)}, u32[]{:S(2)}) collective-permute-start(bf16[5,1,2048]{2,1,0:T(2,128)(2,1)} %get-tuple-element.4), channel_id=1, source_target_pairs={{1,0},{2,1},{3,2},{5,4},{6,5},{7,6},{9,8},{10,9},{11,10},{13,12},{... | collective-permute-start | bytes 61448 | tf_op jit(solution)/shard_map/ppermute | solution.py:50
  133.5 15.5 %copy-start.17 = (bf16[3,8,8,8,128]{4,3,2,1,0:T(8,128)(2,1)S(1)}, bf16[3,8,8,8,128]{4,3,2,1,0:T(8,128)(2,1)}, u32[]{:S(2)}) copy-start(bf16[3,8,8,8,128]{4,3,2,1,0:T(8,128)(2,1)} %get-tuple-element.12) | copy-start | bytes 1179652
  133.6 141.1 %collective-permute-start.14 = (bf16[5,1,2048]{2,1,0:T(2,128)(2,1)}, bf16[5,1,2048]{2,1,0:T(2,128)(2,1)}, u32[]{:S(2)}, u32[]{:S(2)}) collective-permute-start(bf16[5,1,2048]{2,1,0:T(2,128)(2,1)} %get-tuple-element.5), channel_id=1, source_target_pairs={{0,1},{1,2},{2,3},{4,5},{5,6},{6,7},{8,9},{9,10},{10,11},{12,13},{... | collective-permute-start | bytes 61448 | tf_op jit(solution)/shard_map/ppermute | solution.py:49
  144.9 26.5 %all-to-all-start.4 = ((bf16[3,64,1024]{2,0,1:T(4,128)(2,1)}), bf16[3,64,1024]{2,0,1:T(4,128)(2,1)}, u32[]{:S(2)}, u32[]{:S(2)}) async-start(bf16[3,64,1024]{2,0,1:T(4,128)(2,1)} %copy.156), calls=%async_computation.4 | async-start | bytes 1048576 | tf_op jit(solution)/shard_map/all_to_all | solution.py:183
  149.0 124.4 %reduce-scatter.5.cloned.1.call-start = ((), (), s32[]{:S(2)}) async-start(), calls=%async_computation.12 | async-start | bytes 3932160 | tf_op jit(solution)/shard_map/reduce_scatter | solution.py:172
  162.7 102.2 %collective-permute-start.2 = (bf16[5,1,2048]{2,1,0:T(2,128)(2,1)}, bf16[5,1,2048]{2,1,0:T(2,128)(2,1)}, u32[]{:S(2)}, u32[]{:S(2)}) collective-permute-start(bf16[5,1,2048]{2,1,0:T(2,128)(2,1)} %get-tuple-element.6), channel_id=1, source_target_pairs={{0,1},{1,2},{2,3},{4,5},{5,6},{6,7},{8,9},{9,10},{10,11},{12,13},{... | collective-permute-start | bytes 61448 | tf_op jit(solution)/shard_map/ppermute | solution.py:49
  164.6 100.3 %collective-permute-start.3 = (bf16[5,1,2048]{2,1,0:T(2,128)(2,1)}, bf16[5,1,2048]{2,1,0:T(2,128)(2,1)}, u32[]{:S(2)}, u32[]{:S(2)}) collective-permute-start(bf16[5,1,2048]{2,1,0:T(2,128)(2,1)} %get-tuple-element.7), channel_id=1, source_target_pairs={{1,0},{2,1},{3,2},{5,4},{6,5},{7,6},{9,8},{10,9},{11,10},{13,12},{... | collective-permute-start | bytes 61448 | tf_op jit(solution)/shard_map/ppermute | solution.py:50
  171.4 2.5 copy-start.27
  173.9 2.4 copy-start.10
  173.9 2.4 copy-start.12
  174.6 2.8 copy-start.15
  177.4 3.9 %copy-start.18 = (bf16[24,8,8,128]{3,2,1,0:T(8,128)(2,1)S(1)}, bf16[24,8,8,128]{3,2,1,0:T(8,128)(2,1)}, u32[]{:S(2)}) copy-start(bf16[24,8,8,128]{3,2,1,0:T(8,128)(2,1)} %get-tuple-element.48) | copy-start | bytes 1179652
  181.3 2.9 %copy-start.13 = (bf16[24,8,8,128]{3,2,1,0:T(8,128)(2,1)S(1)}, bf16[24,8,8,128]{3,2,1,0:T(8,128)(2,1)}, u32[]{:S(2)}) copy-start(bf16[24,8,8,128]{3,2,1,0:T(8,128)(2,1)} %copy-done.12) | copy-start | bytes 1179652
  183.4 0.8 copy-start.11
  185.7 27.4 %all-to-all-start.6 = ((bf16[24,8,1024]{2,1,0:T(8,128)(2,1)}), bf16[24,8,1024]{2,1,0:T(8,128)(2,1)S(1)}, u32[]{:S(2)}, u32[]{:S(2)}) async-start(bf16[24,8,1024]{2,1,0:T(8,128)(2,1)} %convert_element_type.185), calls=%async_computation.7 | async-start | bytes 786432 | tf_op jit(solution)/shard_map/all_to_all | solution.py:207
  200.1 10.1 %collective-permute-start.4 = (bf16[3,8,1024]{2,1,0:T(8,128)(2,1)}, bf16[3,8,1024]{2,1,0:T(8,128)(2,1)}, u32[]{:S(2)}, u32[]{:S(2)}) collective-permute-start(bf16[3,8,1024]{2,1,0:T(8,128)(2,1)} %get-tuple-element.30), channel_id=1, source_target_pairs={{0,4},{4,0},{8,12},{12,8},{16,20},{20,16},{24,28},{28,24},{1,5},{5... | collective-permute-start | bytes 147464 | tf_op jit(solution)/shard_map/ppermute | solution.py:33
  210.2 7.0 %collective-permute-start.5 = (bf16[3,8,1024]{2,1,0:T(8,128)(2,1)}, bf16[3,8,1024]{2,1,0:T(8,128)(2,1)}, u32[]{:S(2)}, u32[]{:S(2)}) collective-permute-start(bf16[3,8,1024]{2,1,0:T(8,128)(2,1)} %get-tuple-element.29), channel_id=1, source_target_pairs={{0,8},{4,12},{8,0},{12,4},{16,24},{20,28},{24,16},{28,20},{1,9},{5... | collective-permute-start | bytes 147464 | tf_op jit(solution)/shard_map/ppermute | solution.py:33
  213.1 34.5 %all-to-all-start.5 = ((bf16[24,8,1024]{2,1,0:T(8,128)(2,1)}), bf16[24,8,1024]{2,1,0:T(8,128)(2,1)}, u32[]{:S(2)}, u32[]{:S(2)}) async-start(bf16[24,8,1024]{2,1,0:T(8,128)(2,1)} %convert_element_type.181), calls=%async_computation.5 | async-start | bytes 786432 | tf_op jit(solution)/shard_map/all_to_all | solution.py:206
  217.2 8.4 %collective-permute-start.6 = (bf16[3,8,1024]{2,1,0:T(8,128)(2,1)}, bf16[3,8,1024]{2,1,0:T(8,128)(2,1)S(1)}, u32[]{:S(2)}, u32[]{:S(2)}) collective-permute-start(bf16[3,8,1024]{2,1,0:T(8,128)(2,1)} %get-tuple-element.28), channel_id=1, source_target_pairs={{0,12},{4,8},{8,4},{12,0},{16,28},{20,24},{24,20},{28,16},{1,13},{... | collective-permute-start | bytes 147464 | tf_op jit(solution)/shard_map/ppermute | solution.py:33
  225.5 7.3 %collective-permute-start.7 = (bf16[3,8,1024]{2,1,0:T(8,128)(2,1)}, bf16[3,8,1024]{2,1,0:T(8,128)(2,1)S(1)}, u32[]{:S(2)}, u32[]{:S(2)}) collective-permute-start(bf16[3,8,1024]{2,1,0:T(8,128)(2,1)} %get-tuple-element.27), channel_id=1, source_target_pairs={{0,16},{4,20},{8,24},{12,28},{16,0},{20,4},{24,8},{28,12},{1,17},{... | collective-permute-start | bytes 147464 | tf_op jit(solution)/shard_map/ppermute | solution.py:33
  232.8 6.1 %collective-permute-start.8 = (bf16[3,8,1024]{2,1,0:T(8,128)(2,1)}, bf16[3,8,1024]{2,1,0:T(8,128)(2,1)S(1)}, u32[]{:S(2)}, u32[]{:S(2)}) collective-permute-start(bf16[3,8,1024]{2,1,0:T(8,128)(2,1)} %get-tuple-element.26), channel_id=1, source_target_pairs={{0,20},{4,16},{8,28},{12,24},{16,4},{20,0},{24,12},{28,8},{1,21},{... | collective-permute-start | bytes 147464 | tf_op jit(solution)/shard_map/ppermute | solution.py:33
  238.9 6.3 %collective-permute-start.9 = (bf16[3,8,1024]{2,1,0:T(8,128)(2,1)}, bf16[3,8,1024]{2,1,0:T(8,128)(2,1)}, u32[]{:S(2)}, u32[]{:S(2)}) collective-permute-start(bf16[3,8,1024]{2,1,0:T(8,128)(2,1)} %get-tuple-element.25), channel_id=1, source_target_pairs={{0,24},{4,28},{8,16},{12,20},{16,8},{20,12},{24,0},{28,4},{1,25},{... | collective-permute-start | bytes 147464 | tf_op jit(solution)/shard_map/ppermute | solution.py:33
  245.2 7.8 %collective-permute-start.10 = (bf16[3,8,1024]{2,1,0:T(8,128)(2,1)}, bf16[3,8,1024]{2,1,0:T(8,128)(2,1)}, u32[]{:S(2)}, u32[]{:S(2)}) collective-permute-start(bf16[3,8,1024]{2,1,0:T(8,128)(2,1)} %get-tuple-element.24), channel_id=1, source_target_pairs={{0,28},{4,24},{8,20},{12,16},{16,12},{20,8},{24,4},{28,0},{1,29},{... | collective-permute-start | bytes 147464 | tf_op jit(solution)/shard_map/ppermute | solution.py:33
  247.5 13.3 %all-to-all-start.3 = ((bf16[24,8,1024]{2,1,0:T(8,128)(2,1)}), bf16[24,8,1024]{2,1,0:T(8,128)(2,1)}, u32[]{:S(2)}, u32[]{:S(2)}) async-start(bf16[24,8,1024]{2,1,0:T(8,128)(2,1)} %convert_element_type.159), calls=%async_computation.3 | async-start | bytes 786432 | tf_op jit(solution)/shard_map/all_to_all | solution.py:205
  263.7 1.1 copy-start.16
  263.7 1.3 copy-start.19
  263.7 1.3 copy-start.20
  263.7 1.3 copy-start.21
  263.7 1.3 copy-start.22
  263.7 1.3 copy-start.23
  263.8 1.3 copy-start.24
  263.8 1.3 copy-start.25
  263.8 1.3 copy-start.26
  265.0 7.4 %copy-start.9 = (bf16[3,8,8,1024]{3,2,1,0:T(8,128)(2,1)S(1)}, bf16[3,8,8,1024]{3,2,1,0:T(8,128)(2,1)}, u32[]{:S(2)}) copy-start(bf16[3,8,8,1024]{3,2,1,0:T(8,128)(2,1)} %copy.217) | copy-start | bytes 1179652
  272.5 2.2 copy-start.7
Sparse Core Ops, SparseCore 0:
  10.2 22.3 all-gather.2
  34.7 19.6 all-gather.4
  72.3 37.9 reduce-scatter.2
  159.5 38.3 reduce-scatter.4
